TPU v7x, 32 devices: a whole 2x2x4 slice. The times are simulated.
32 devices in a mesh: grp: 4 (over y, x), blk: 8 (over z, core).
Axes of the slice: x: 2, y: 2, z: 4, core: 2. Of those that a mesh axis runs over, the one named last changes fastest.
Arguments:
- estimate: float32 [32, 256, 256], P('blk'), may hold values from 0.25 to 4
- measured: bfloat16 [6, 256, 32, 256], P(None, 'blk'), may hold values from 0.25 to 4
- tile_plane: int32 [6, 256], P(None, 'blk'), may hold values from 0 to 31, as said below
- tile_strip: int32 [6, 256], P(None, 'blk'), may hold values from 0 to 7, as said below
- view_group: int32 [6], replicated, may hold values from 0 to 3, as said below
- kernel_cols: float32 [6, 3, 31], replicated, may hold values from 0.002 to 0.1
- kernel_rows: float32 [6, 3, 31], replicated, may hold values from 0.002 to 0.1
- kernel_planes: float32 [6, 3, 31], replicated, may hold values from 0.002 to 0.1
Outputs:
- updated: float32 [32, 256, 256], P('blk')
Inputs may be any that keep to these rules, and one draw needn't show every extreme that they name: For each view the pairs (tile_plane, tile_strip) name every plane and strip exactly once; the 32 tiles of one view on one device of blk hold exactly 4 tiles of every block of 4 consecutive planes and exactly 4 tiles of every strip. `tile_strip`: see tile_plane. `view_group`: every group has at least one view and at most 2; some group has exactly 2.
All inputs are finite; a program needn't handle non-finite values.
Results may differ from a plain program's by a relative error of at most 0.0003.
Values may be sent and summed in bfloat16 or wider, within the bound.
A program may use at most 128 MiB of HBM per device.

v0:
```python
import jax
import jax.numpy as jnp
from jax import lax
from jax.sharding import PartitionSpec as P

VSLOT = 2
HIGH = lax.Precision.HIGH


def band(taps, rows, cols, lead):
    width = taps.shape[-1]
    shift = lax.broadcasted_iota(jnp.int32, (rows, cols), 1) - lax.broadcasted_iota(
        jnp.int32, (rows, cols), 0
    )
    shift = shift - lead + width // 2
    out = jnp.zeros(taps.shape[:-1] + (rows, cols), jnp.float32)
    for t in range(width):
        out = jnp.where(shift == t, taps[..., t, None, None], out)
    return out


def shards(
    estimate, measured, tile_plane, tile_strip, view_group, kernel_cols, kernel_rows, kernel_planes
):
    cz, ny, nx = estimate.shape
    blocks = lax.axis_size("blk")
    groups = lax.axis_size("grp")
    nz = cz * blocks
    py = ny // blocks
    half = kernel_rows.shape[-1] // 2
    lead = -(-half // 8) * 8
    ext = py + 2 * lead
    tiles = measured.shape[1]
    per = tiles // blocks
    matches = (view_group == lax.axis_index("grp")).astype(jnp.int32)
    ranking = jnp.cumsum(matches) - matches
    members = jnp.sum(matches).astype(jnp.float32)
    ids = jnp.arange(view_group.shape[0], dtype=jnp.int32)
    picked = [matches * (ranking == s).astype(jnp.int32) for s in range(VSLOT)]
    chosen = [jnp.sum(p * ids) for p in picked]
    weights = jnp.stack([jnp.sum(p).astype(jnp.float32) / members for p in picked])
    padded = jnp.pad(estimate, ((0, 0), (lead, lead), (0, 0)))
    windows = jnp.stack([padded[:, j * py : j * py + ext] for j in range(blocks)])
    pencil = lax.all_to_all(windows, "blk", 0, 0, tiled=True).reshape(nz, ext, nx)
    pick = lambda a: jnp.stack([lax.dynamic_index_in_dim(a, c, 0, keepdims=False) for c in chosen])
    pieces, planes, strips = (pick(measured), pick(tile_plane), pick(tile_strip))
    hits = (strips[:, :, None] == jnp.arange(blocks, dtype=jnp.int32)).astype(jnp.int32)
    before = jnp.cumsum(hits, axis=1) - hits
    positions = strips * per + jnp.sum(before * hits, axis=2)
    order = positions[:, None, :] == jnp.arange(tiles, dtype=jnp.int32)[None, :, None]
    send_planes = jnp.sum(jnp.where(order, planes[:, None, :], 0), axis=2)
    send = jnp.einsum("vpi,viyx->pvyx", order.astype(jnp.bfloat16), pieces)
    got = lax.all_to_all(send, "blk", 0, 0, tiled=True)
    got_planes = lax.all_to_all(send_planes.T, "blk", 0, 0, tiled=True)
    place = (got_planes[None] == jnp.arange(nz, dtype=jnp.int32)[:, None, None]).astype(
        jnp.bfloat16
    )
    observed = jnp.einsum("ptv,tvyx->vpyx", place, got).astype(jnp.float32)
    kc, kr, kp = (pick(kernel_cols), pick(kernel_rows), pick(kernel_planes))
    bx = band(kc, nx, nx, 0)
    by = band(kr, py, ext, lead)
    bz = band(kp, nz, nz, 0)
    byw = by * weights[:, None, None, None]
    t = jnp.einsum("zmx,vrim->vrzix", pencil, by, precision=HIGH)
    t = jnp.einsum("vrzix,vrnx->vrzin", t, bx, precision=HIGH)
    blurred = jnp.einsum("vrzin,vrpz->vpin", t, bz, precision=HIGH)
    ratios = observed / blurred
    a = jnp.einsum("vpin,vrpz->vrzin", ratios, bz, precision=HIGH)
    a = jnp.einsum("vrzin,vrnx->vrzix", a, bx, precision=HIGH)
    wide = jnp.einsum("vrzix,vrim->zmx", a, byw, precision=HIGH)
    chunk = min(py, lead)
    average = wide[:, lead : lead + py]
    for d in range(1, lead // chunk + 1):
        up = wide[:, lead + py + (d - 1) * chunk : lead + py + d * chunk]
        down = wide[:, lead - d * chunk : lead - (d - 1) * chunk]
        up = lax.ppermute(up, "blk", [(i, i + d) for i in range(blocks - d)])
        down = lax.ppermute(down, "blk", [(i, i - d) for i in range(d, blocks)])
        rest = py - chunk
        average = (
            average
            + jnp.pad(up, ((0, 0), (0, rest), (0, 0)))
            + jnp.pad(down, ((0, 0), (rest, 0), (0, 0)))
        )
    logs = jnp.log(average)
    logs = lax.all_to_all(logs.reshape(blocks, cz, py, nx), "blk", 0, 0, tiled=True)
    summed = lax.psum(logs, "grp")
    summed = jnp.transpose(summed, (1, 0, 2, 3)).reshape(cz, ny, nx)
    return estimate * jnp.exp(summed / groups)


def solution(mesh):
    in_specs = (
        P("blk", None, None),
        P(None, "blk", None, None),
        P(None, "blk"),
        P(None, "blk"),
        P(),
        P(),
        P(),
        P(),
    )
    return jax.shard_map(
        shards, mesh=mesh, in_specs=in_specs, out_specs=P("blk", None, None), check_vma=False
    )
```

profile of v0, /device:TPU:0, one launch (start us, length us, event | category | flops | bytes accessed | tf_op | source)
XLA Modules:
  0.0 310.7 jit_solution(15629209679689618100)
XLA Ops:
  7.4 1.4 fusion.249
  12.8 0.8 constant_dynamic-slice_fusion.7
  13.5 0.8 constant_dynamic-slice_fusion.5
  15.5 6.4 %all-to-all-start = ((s32[8,4,2]{1,2,0:T(2,128)}), s32[8,4,2]{1,2,0:T(2,128)S(1)}, u32[]{:S(2)}, u32[]{:S(2)}) async-start(s32[8,4,2]{1,2,0:T(2,128)} %copy.106), calls=%async_computation | async-start | bytes 16384 | tf_op jit(solution)/shard_map/all_to_all | solution.py:54
  21.8 0.7 constant_dynamic-slice_fusion.11
  31.4 0.7 constant_dynamic-slice_fusion.1
  32.4 0.8 fusion.160
  33.2 0.8 fusion.178
  34.0 0.8 fusion.196
  34.7 0.8 fusion.214
  44.3 0.7 copy.186
  47.7 0.7 copy.191
  51.8 0.7 copy.171
  53.2 0.7 copy.173
  55.2 0.7 copy.195
  57.3 0.7 copy.202
  62.1 0.7 copy.209
  62.8 0.7 copy.210
  64.9 0.7 copy.213
  73.8 0.7 copy.226
  75.8 0.7 copy.229
  77.9 1.3 constant_dynamic-slice_fusion.3
  80.2 1.6 copy.110
  84.4 5.1 %all-to-all-start.1 = ((bf16[32,2,32,256]{3,2,1,0:T(8,128)(2,1)}), bf16[32,2,32,256]{3,2,1,0:T(8,128)(2,1)S(1)}, u32[]{:S(2)}, u32[]{:S(2)}) async-start(bf16[32,2,32,256]{3,2,1,0:T(8,128)(2,1)} %copy.110), calls=%async_computation.1 | async-start | bytes 2097152 | tf_op jit(solution)/shard_map/all_to_all | solution.py:53
  89.6 0.7 fusion.17
  90.3 0.7 bitcast_dynamic-update-slice_fusion.5
  91.0 0.7 bitcast_dynamic-update-slice_fusion.4
  91.8 0.7 bitcast_dynamic-update-slice_fusion.3
  92.5 0.7 bitcast_dynamic-update-slice_fusion.2
  93.2 0.7 bitcast_dynamic-update-slice_fusion.1
  93.9 0.7 bitcast_dynamic-update-slice_fusion
  94.6 0.7 fusion.19
  95.4 20.7 %all-to-all-done.1 = bf16[32,2,32,256]{3,2,1,0:T(8,128)(2,1)S(1)} async-done(((bf16[32,2,32,256]{3,2,1,0:T(8,128)(2,1)}), bf16[32,2,32,256]{3,2,1,0:T(8,128)(2,1)S(1)}, u32[]{:S(2)}, u32[]{:S(2)}) %all-to-all-start.1) | async-done | bytes 1048608 | tf_op jit(solution)/shard_map/all_to_all | solution.py:53
  116.1 1.0 copy-done.2
  117.1 3.6 %all-to-all-start.2 = ((f32[8,4,64,256]{3,2,1,0:T(8,128)}), f32[8,4,64,256]{3,2,1,0:T(8,128)S(1)}, u32[]{:S(2)}, u32[]{:S(2)}) async-start(f32[8,4,64,256]{3,2,1,0:T(8,128)} %fusion.19), calls=%async_computation.2 | async-start | bytes 4194304 | tf_op jit(solution)/shard_map/all_to_all | solution.py:44
  122.8 0.7 fusion.24
  123.5 0.7 fusion.26
  124.2 0.7 fusion.28
  124.9 0.7 fusion.30
  125.7 0.7 fusion.32
  126.4 0.7 fusion.34
  127.1 0.7 fusion.36
  127.8 0.7 fusion.38
  128.5 0.7 fusion.40
  129.2 0.7 fusion.42
  130.0 0.7 fusion.44
  130.7 0.7 fusion.46
  131.4 0.7 fusion.48
  132.7 1.4 eq.730
  134.0 2.9 fusion.14
  137.0 32.7 %all-to-all-done.2 = f32[8,4,64,256]{3,2,1,0:T(8,128)S(1)} async-done(((f32[8,4,64,256]{3,2,1,0:T(8,128)}), f32[8,4,64,256]{3,2,1,0:T(8,128)S(1)}, u32[]{:S(2)}, u32[]{:S(2)}) %all-to-all-start.2) | async-done | bytes 2097184 | tf_op jit(solution)/shard_map/all_to_all | solution.py:44
  169.9 4.2 %convolution_bitcast_fusion = f32[2,3,32,32,256]{4,3,2,1,0:T(8,128)S(1)} fusion(f32[32,64,256,1,1]{2,1,0,4,3:T(8,128)S(1)} %bitcast.177, f32[2,3]{0,1:T(4,128)} %bitcast.239, pred[32,64]{1,0:T(8,128)(4,1)S(1)} %get-tuple-element.121, f32[2,3]{0,1:T(4,128)} %bitcast.237, pred[32,64]{1,0:T(8,128)(4,1)S(1)} %get-tuple-element.122, f32[2,3]{0,1:T(4,128)} %bitcast.235, ...), kind=kOutput, calls=%fused_computation.4 | convolution fusion | flops 604360704 | bytes 8452840 | tf_op jit(solution)/shard_map/zmx,vrim->vrzix/dot_general | solution.py:64
  174.5 10.7 %fusion.2 = f32[2,3,32,32,256]{4,2,1,3,0:T(8,128)S(1)} fusion(f32[2,3,32,32,256]{4,3,2,1,0:T(8,128)S(1)} %convolution_bitcast_fusion, f32[2,3]{0,1:T(4,128)} %bitcast.302, pred[256,256]{1,0:T(8,128)(4,1)S(1)} %get-tuple-element.151, f32[2,3]{0,1:T(4,128)} %bitcast.300, pred[256,256]{1,0:T(8,128)(4,1)S(1)} %get-tuple-element.152, f32[2,3]{0,1:T(4,128)} %bitcast.298, ...), kind=kOutput, calls=%fused_computation.2 | convolution fusion | flops 2428108800 | bytes 14615272 | tf_op jit(solution)/shard_map/vrzix,vrnx->vrzin/dot_general | solution.py:65
  185.6 3.2 %fusion.51 = f32[2,32,32,256,1]{3,1,4,2,0:T(8,128)S(1)} fusion(f32[2,3,32,32,256]{4,2,1,3,0:T(8,128)S(1)} %fusion.2, f32[2,3]{1,0:T(2,128)} %get-tuple-element.34, f32[2,3]{1,0:T(2,128)} %get-tuple-element.35, f32[2,3]{1,0:T(2,128)} %get-tuple-element.33, f32[2,3]{1,0:T(2,128)} %get-tuple-element.32, f32[2,3]{1,0:T(2,128)} %get-tuple-element.31, ...), kind=kOutput, calls=%fused_computation.68 | convolution fusion | flops 302180352 | bytes 8421096 | tf_op jit(solution)/shard_map/vrzin,vrpz->vpin/dot_general | solution.py:66
  189.0 2.9 fusion.4
  192.4 11.0 %fusion = f32[2,3,32,32,256]{4,3,0,2,1:T(8,128)S(1)} fusion(f32[2,3,32,32,256]{4,2,3,1,0:T(8,128)S(1)} %fusion.4, f32[2,3]{0,1:T(4,128)} %bitcast.303, f32[2,3]{0,1:T(4,128)} %bitcast.301, f32[2,3]{0,1:T(4,128)} %bitcast.299, f32[2,3]{0,1:T(4,128)} %bitcast.297, f32[2,3]{0,1:T(4,128)} %bitcast.295, f32[2,3]{0,1:T(4,128)} %bitcast.293, f32[2,3]{0,1:T(4,128)} %bitcast.291, ...), kind=kOutput, calls=%fused_computation | convolution fusion | flops 2428108800 | bytes 14615272 | tf_op jit(solution)/shard_map/vrzin,vrnx->vrzix/dot_general | solution.py:69
  203.7 3.6 %convolution_bitcast_fusion.1 = f32[32,64,256]{2,1,0:T(8,128)S(1)} fusion(f32[2,3,32,32,256]{4,3,0,2,1:T(8,128)S(1)} %fusion, f32[2]{0:T(128)} %pad_maximum_fusion.3, f32[2,3]{0,1:T(4,128)} %bitcast.240, f32[2,3]{0,1:T(4,128)} %bitcast.238, f32[2,3]{0,1:T(4,128)} %bitcast.236, f32[2,3]{0,1:T(4,128)} %bitcast.234, f32[2,3]{0,1:T(4,128)} %bitcast.218, ...), kind=kOutput, calls=%fused_computation.9 | convolution fusion | flops 604372992 | bytes 8452848 | tf_op jit(solution)/shard_map/vrzix,vrim->zmx/dot_general | solution.py:70
  207.4 1.5 collective-permute-start
  208.9 1.3 collective-permute-start.1
  210.4 2.3 collective-permute-done.1
  213.0 36.4 %all_to_all.24 = f32[8,4,32,256]{3,2,1,0:T(8,128)} all-to-all(f32[8,4,32,256]{3,2,1,0:T(8,128)S(1)} %bitcast.178), channel_id=1, replica_groups=mesh['grp'=4,'blk'=8] {'blk'}, dimensions={0} | all-to-all | bytes 2097152 | tf_op jit(solution)/shard_map/all_to_all | solution.py:85
  249.4 51.6 %all-reduce.5.cloned.1.call-done = f32[8,4,32,256]{3,2,1,0:T(8,128)} async-done(((f32[8,4,32,256]{3,2,1,0:T(8,128)}), f32[8,4,32,256]{3,2,1,0:T(8,128)}) %all-reduce.5.cloned.1.call-update) | async-done | bytes 1048592 | tf_op jit(solution)/shard_map/psum | solution.py:86
  301.1 1.4 exponential_bitcast_fusion
  302.5 1.1 bitcast_multiply_fusion
  (321 shorter events, 51.1 us)
Async XLA Ops:
  15.5 68.4 %all-to-all-start = ((s32[8,4,2]{1,2,0:T(2,128)}), s32[8,4,2]{1,2,0:T(2,128)S(1)}, u32[]{:S(2)}, u32[]{:S(2)}) async-start(s32[8,4,2]{1,2,0:T(2,128)} %copy.106), calls=%async_computation | async-start | bytes 16384 | tf_op jit(solution)/shard_map/all_to_all | solution.py:54
  81.7 7.8 %copy-start = (f32[4,256,256]{2,1,0:T(8,128)S(1)}, f32[4,256,256]{2,1,0:T(8,128)}, u32[]{:S(2)}) copy-start(f32[4,256,256]{2,1,0:T(8,128)} %param.8) | copy-start | bytes 3145732
  84.4 31.7 %all-to-all-start.1 = ((bf16[32,2,32,256]{3,2,1,0:T(8,128)(2,1)}), bf16[32,2,32,256]{3,2,1,0:T(8,128)(2,1)S(1)}, u32[]{:S(2)}, u32[]{:S(2)}) async-start(bf16[32,2,32,256]{3,2,1,0:T(8,128)(2,1)} %copy.110), calls=%async_computation.1 | async-start | bytes 2097152 | tf_op jit(solution)/shard_map/all_to_all | solution.py:53
  117.1 52.6 %all-to-all-start.2 = ((f32[8,4,64,256]{3,2,1,0:T(8,128)}), f32[8,4,64,256]{3,2,1,0:T(8,128)S(1)}, u32[]{:S(2)}, u32[]{:S(2)}) async-start(f32[8,4,64,256]{3,2,1,0:T(8,128)} %fusion.19), calls=%async_computation.2 | async-start | bytes 4194304 | tf_op jit(solution)/shard_map/all_to_all | solution.py:44
  120.7 180.4 %all-reduce.5.cloned.1.call-start = ((), (), s32[]{:S(2)}) async-start(), calls=%async_computation.4 | async-start | bytes 2097152 | tf_op jit(solution)/shard_map/psum | solution.py:86
  121.2 10.9 %copy-start.57 = (s32[8,4,2]{1,2,0:T(2,128)S(1)}, s32[8,4,2]{1,2,0:T(2,128)}, u32[]{:S(2)}) copy-start(s32[8,4,2]{1,2,0:T(2,128)} %copy-done.56) | copy-start | bytes 772
  169.7 4.5 %copy-start.7 = (pred[256,256]{1,0:T(8,128)(4,1)S(1)}, pred[256,256]{1,0:T(8,128)(4,1)}, u32[]{:S(2)}) copy-start(pred[256,256]{1,0:T(8,128)(4,1)} %get-tuple-element.158) | copy-start | bytes 196612
  169.7 4.5 %copy-start.8 = (pred[256,256]{1,0:T(8,128)(4,1)S(1)}, pred[256,256]{1,0:T(8,128)(4,1)}, u32[]{:S(2)}) copy-start(pred[256,256]{1,0:T(8,128)(4,1)} %get-tuple-element.159) | copy-start | bytes 196612
  169.7 4.5 %copy-start.9 = (pred[256,256]{1,0:T(8,128)(4,1)S(1)}, pred[256,256]{1,0:T(8,128)(4,1)}, u32[]{:S(2)}) copy-start(pred[256,256]{1,0:T(8,128)(4,1)} %get-tuple-element.160) | copy-start | bytes 196612
  169.7 4.5 %copy-start.10 = (pred[256,256]{1,0:T(8,128)(4,1)S(1)}, pred[256,256]{1,0:T(8,128)(4,1)}, u32[]{:S(2)}) copy-start(pred[256,256]{1,0:T(8,128)(4,1)} %get-tuple-element.161) | copy-start | bytes 196612
  169.7 4.5 %copy-start.11 = (pred[256,256]{1,0:T(8,128)(4,1)S(1)}, pred[256,256]{1,0:T(8,128)(4,1)}, u32[]{:S(2)}) copy-start(pred[256,256]{1,0:T(8,128)(4,1)} %get-tuple-element.162) | copy-start | bytes 196612
  174.4 10.9 %copy-start.71 = (f32[2,3]{1,0:T(2,128)S(1)}, f32[2,3]{1,0:T(2,128)}, u32[]{:S(2)}) copy-start(f32[2,3]{1,0:T(2,128)} %get-tuple-element.5) | copy-start | bytes 76
  174.4 10.9 %copy-start.72 = (f32[2,3]{1,0:T(2,128)S(1)}, f32[2,3]{1,0:T(2,128)}, u32[]{:S(2)}) copy-start(f32[2,3]{1,0:T(2,128)} %get-tuple-element.6) | copy-start | bytes 76
  174.4 10.9 %copy-start.73 = (f32[2,3]{1,0:T(2,128)S(1)}, f32[2,3]{1,0:T(2,128)}, u32[]{:S(2)}) copy-start(f32[2,3]{1,0:T(2,128)} %get-tuple-element.7) | copy-start | bytes 76
  174.4 10.9 %copy-start.74 = (f32[2,3]{1,0:T(2,128)S(1)}, f32[2,3]{1,0:T(2,128)}, u32[]{:S(2)}) copy-start(f32[2,3]{1,0:T(2,128)} %get-tuple-element.8) | copy-start | bytes 76
  174.4 10.9 %copy-start.75 = (f32[2,3]{1,0:T(2,128)S(1)}, f32[2,3]{1,0:T(2,128)}, u32[]{:S(2)}) copy-start(f32[2,3]{1,0:T(2,128)} %get-tuple-element.9) | copy-start | bytes 76
  174.4 10.9 %copy-start.76 = (f32[2,3]{1,0:T(2,128)S(1)}, f32[2,3]{1,0:T(2,128)}, u32[]{:S(2)}) copy-start(f32[2,3]{1,0:T(2,128)} %get-tuple-element.10) | copy-start | bytes 76
  174.4 10.9 %copy-start.77 = (f32[2,3]{1,0:T(2,128)S(1)}, f32[2,3]{1,0:T(2,128)}, u32[]{:S(2)}) copy-start(f32[2,3]{1,0:T(2,128)} %get-tuple-element.11) | copy-start | bytes 76
  174.5 10.9 %copy-start.78 = (f32[2,3]{1,0:T(2,128)S(1)}, f32[2,3]{1,0:T(2,128)}, u32[]{:S(2)}) copy-start(f32[2,3]{1,0:T(2,128)} %get-tuple-element.12) | copy-start | bytes 76
  174.5 10.9 %copy-start.79 = (f32[2,3]{1,0:T(2,128)S(1)}, f32[2,3]{1,0:T(2,128)}, u32[]{:S(2)}) copy-start(f32[2,3]{1,0:T(2,128)} %get-tuple-element.13) | copy-start | bytes 76
  174.5 10.9 %copy-start.80 = (f32[2,3]{1,0:T(2,128)S(1)}, f32[2,3]{1,0:T(2,128)}, u32[]{:S(2)}) copy-start(f32[2,3]{1,0:T(2,128)} %get-tuple-element.14) | copy-start | bytes 76
  174.5 10.9 %copy-start.81 = (f32[2,3]{1,0:T(2,128)S(1)}, f32[2,3]{1,0:T(2,128)}, u32[]{:S(2)}) copy-start(f32[2,3]{1,0:T(2,128)} %get-tuple-element.15) | copy-start | bytes 76
  174.5 10.9 %copy-start.82 = (f32[2,3]{1,0:T(2,128)S(1)}, f32[2,3]{1,0:T(2,128)}, u32[]{:S(2)}) copy-start(f32[2,3]{1,0:T(2,128)} %get-tuple-element.16) | copy-start | bytes 76
  192.0 11.4 %copy-start.30 = (pred[32,64]{1,0:T(8,128)(4,1)S(1)}, pred[32,64]{1,0:T(8,128)(4,1)}, u32[]{:S(2)}) copy-start(pred[32,64]{1,0:T(8,128)(4,1)} %get-tuple-element.126) | copy-start | bytes 6148
  192.0 11.4 %copy-start.31 = (pred[32,64]{1,0:T(8,128)(4,1)S(1)}, pred[32,64]{1,0:T(8,128)(4,1)}, u32[]{:S(2)}) copy-start(pred[32,64]{1,0:T(8,128)(4,1)} %get-tuple-element.127) | copy-start | bytes 6148
  192.0 11.4 %copy-start.32 = (pred[32,64]{1,0:T(8,128)(4,1)S(1)}, pred[32,64]{1,0:T(8,128)(4,1)}, u32[]{:S(2)}) copy-start(pred[32,64]{1,0:T(8,128)(4,1)} %get-tuple-element.128) | copy-start | bytes 6148
  192.0 11.4 %copy-start.33 = (pred[32,64]{1,0:T(8,128)(4,1)S(1)}, pred[32,64]{1,0:T(8,128)(4,1)}, u32[]{:S(2)}) copy-start(pred[32,64]{1,0:T(8,128)(4,1)} %get-tuple-element.129) | copy-start | bytes 6148
  192.0 11.4 %copy-start.34 = (pred[32,64]{1,0:T(8,128)(4,1)S(1)}, pred[32,64]{1,0:T(8,128)(4,1)}, u32[]{:S(2)}) copy-start(pred[32,64]{1,0:T(8,128)(4,1)} %get-tuple-element.130) | copy-start | bytes 6148
  192.0 11.4 %copy-start.35 = (pred[32,64]{1,0:T(8,128)(4,1)S(1)}, pred[32,64]{1,0:T(8,128)(4,1)}, u32[]{:S(2)}) copy-start(pred[32,64]{1,0:T(8,128)(4,1)} %get-tuple-element.131) | copy-start | bytes 6148
  192.0 11.4 %copy-start.36 = (pred[32,64]{1,0:T(8,128)(4,1)S(1)}, pred[32,64]{1,0:T(8,128)(4,1)}, u32[]{:S(2)}) copy-start(pred[32,64]{1,0:T(8,128)(4,1)} %get-tuple-element.132) | copy-start | bytes 6148
  192.0 11.4 %copy-start.37 = (pred[32,64]{1,0:T(8,128)(4,1)S(1)}, pred[32,64]{1,0:T(8,128)(4,1)}, u32[]{:S(2)}) copy-start(pred[32,64]{1,0:T(8,128)(4,1)} %get-tuple-element.133) | copy-start | bytes 6148
  192.0 11.4 %copy-start.38 = (pred[32,64]{1,0:T(8,128)(4,1)S(1)}, pred[32,64]{1,0:T(8,128)(4,1)}, u32[]{:S(2)}) copy-start(pred[32,64]{1,0:T(8,128)(4,1)} %get-tuple-element.134) | copy-start | bytes 6148
  192.1 11.4 %copy-start.39 = (pred[32,64]{1,0:T(8,128)(4,1)S(1)}, pred[32,64]{1,0:T(8,128)(4,1)}, u32[]{:S(2)}) copy-start(pred[32,64]{1,0:T(8,128)(4,1)} %get-tuple-element.135) | copy-start | bytes 6148
  192.1 11.4 %copy-start.40 = (pred[32,64]{1,0:T(8,128)(4,1)S(1)}, pred[32,64]{1,0:T(8,128)(4,1)}, u32[]{:S(2)}) copy-start(pred[32,64]{1,0:T(8,128)(4,1)} %get-tuple-element.136) | copy-start | bytes 6148
  192.1 11.4 %copy-start.41 = (pred[32,64]{1,0:T(8,128)(4,1)S(1)}, pred[32,64]{1,0:T(8,128)(4,1)}, u32[]{:S(2)}) copy-start(pred[32,64]{1,0:T(8,128)(4,1)} %get-tuple-element.137) | copy-start | bytes 6148
  192.1 11.4 %copy-start.42 = (pred[32,64]{1,0:T(8,128)(4,1)S(1)}, pred[32,64]{1,0:T(8,128)(4,1)}, u32[]{:S(2)}) copy-start(pred[32,64]{1,0:T(8,128)(4,1)} %get-tuple-element.138) | copy-start | bytes 6148
  192.1 11.4 %copy-start.43 = (pred[32,64]{1,0:T(8,128)(4,1)S(1)}, pred[32,64]{1,0:T(8,128)(4,1)}, u32[]{:S(2)}) copy-start(pred[32,64]{1,0:T(8,128)(4,1)} %get-tuple-element.139) | copy-start | bytes 6148
  192.1 11.4 %copy-start.44 = (pred[32,64]{1,0:T(8,128)(4,1)S(1)}, pred[32,64]{1,0:T(8,128)(4,1)}, u32[]{:S(2)}) copy-start(pred[32,64]{1,0:T(8,128)(4,1)} %get-tuple-element.140) | copy-start | bytes 6148
  192.1 11.4 %copy-start.45 = (pred[32,64]{1,0:T(8,128)(4,1)S(1)}, pred[32,64]{1,0:T(8,128)(4,1)}, u32[]{:S(2)}) copy-start(pred[32,64]{1,0:T(8,128)(4,1)} %get-tuple-element.141) | copy-start | bytes 6148
  192.1 11.4 %copy-start.46 = (pred[32,64]{1,0:T(8,128)(4,1)S(1)}, pred[32,64]{1,0:T(8,128)(4,1)}, u32[]{:S(2)}) copy-start(pred[32,64]{1,0:T(8,128)(4,1)} %get-tuple-element.142) | copy-start | bytes 6148
  192.1 11.4 %copy-start.47 = (pred[32,64]{1,0:T(8,128)(4,1)S(1)}, pred[32,64]{1,0:T(8,128)(4,1)}, u32[]{:S(2)}) copy-start(pred[32,64]{1,0:T(8,128)(4,1)} %get-tuple-element.143) | copy-start | bytes 6148
  192.1 11.4 %copy-start.48 = (pred[32,64]{1,0:T(8,128)(4,1)S(1)}, pred[32,64]{1,0:T(8,128)(4,1)}, u32[]{:S(2)}) copy-start(pred[32,64]{1,0:T(8,128)(4,1)} %get-tuple-element.144) | copy-start | bytes 6148
  192.2 11.4 %copy-start.49 = (pred[32,64]{1,0:T(8,128)(4,1)S(1)}, pred[32,64]{1,0:T(8,128)(4,1)}, u32[]{:S(2)}) copy-start(pred[32,64]{1,0:T(8,128)(4,1)} %get-tuple-element.145) | copy-start | bytes 6148
  192.2 11.4 %copy-start.50 = (pred[32,64]{1,0:T(8,128)(4,1)S(1)}, pred[32,64]{1,0:T(8,128)(4,1)}, u32[]{:S(2)}) copy-start(pred[32,64]{1,0:T(8,128)(4,1)} %get-tuple-element.146) | copy-start | bytes 6148
  192.2 11.4 %copy-start.51 = (pred[32,64]{1,0:T(8,128)(4,1)S(1)}, pred[32,64]{1,0:T(8,128)(4,1)}, u32[]{:S(2)}) copy-start(pred[32,64]{1,0:T(8,128)(4,1)} %get-tuple-element.147) | copy-start | bytes 6148
  192.2 11.4 %copy-start.52 = (pred[32,64]{1,0:T(8,128)(4,1)S(1)}, pred[32,64]{1,0:T(8,128)(4,1)}, u32[]{:S(2)}) copy-start(pred[32,64]{1,0:T(8,128)(4,1)} %get-tuple-element.148) | copy-start | bytes 6148
  192.2 11.4 %copy-start.53 = (pred[32,64]{1,0:T(8,128)(4,1)S(1)}, pred[32,64]{1,0:T(8,128)(4,1)}, u32[]{:S(2)}) copy-start(pred[32,64]{1,0:T(8,128)(4,1)} %get-tuple-element.149) | copy-start | bytes 6148
  192.2 11.4 %copy-start.54 = (pred[32,64]{1,0:T(8,128)(4,1)S(1)}, pred[32,64]{1,0:T(8,128)(4,1)}, u32[]{:S(2)}) copy-start(pred[32,64]{1,0:T(8,128)(4,1)} %get-tuple-element.150) | copy-start | bytes 6148
  192.2 11.4 %copy-start.55 = (pred[32,64]{1,0:T(8,128)(4,1)S(1)}, pred[32,64]{1,0:T(8,128)(4,1)}, u32[]{:S(2)}) copy-start(pred[32,64]{1,0:T(8,128)(4,1)} %fusion.126) | copy-start | bytes 6148
  192.2 11.4 %copy-start.58 = (f32[2,3,1]{0,1,2:T(4,128)S(1)}, f32[2,3,1]{0,1,2:T(4,128)}, u32[]{:S(2)}) copy-start(f32[2,3,1]{0,1,2:T(4,128)} %copy.174) | copy-start | bytes 76
  192.2 11.4 %copy-start.59 = (f32[2,3,1]{0,1,2:T(4,128)S(1)}, f32[2,3,1]{0,1,2:T(4,128)}, u32[]{:S(2)}) copy-start(f32[2,3,1]{0,1,2:T(4,128)} %copy.175) | copy-start | bytes 76
  192.2 11.4 %copy-start.60 = (f32[2,3,1]{0,1,2:T(4,128)S(1)}, f32[2,3,1]{0,1,2:T(4,128)}, u32[]{:S(2)}) copy-start(f32[2,3,1]{0,1,2:T(4,128)} %copy.176) | copy-start | bytes 76
  192.3 11.4 %copy-start.61 = (f32[2,3,1]{0,1,2:T(4,128)S(1)}, f32[2,3,1]{0,1,2:T(4,128)}, u32[]{:S(2)}) copy-start(f32[2,3,1]{0,1,2:T(4,128)} %copy.177) | copy-start | bytes 76
  192.3 11.4 %copy-start.62 = (f32[2,3,1]{0,1,2:T(4,128)S(1)}, f32[2,3,1]{0,1,2:T(4,128)}, u32[]{:S(2)}) copy-start(f32[2,3,1]{0,1,2:T(4,128)} %copy.178) | copy-start | bytes 76
  192.3 11.4 %copy-start.63 = (f32[2,3,1]{0,1,2:T(4,128)S(1)}, f32[2,3,1]{0,1,2:T(4,128)}, u32[]{:S(2)}) copy-start(f32[2,3,1]{0,1,2:T(4,128)} %copy.179) | copy-start | bytes 76
  192.3 11.4 %copy-start.64 = (f32[2,3,1]{0,1,2:T(4,128)S(1)}, f32[2,3,1]{0,1,2:T(4,128)}, u32[]{:S(2)}) copy-start(f32[2,3,1]{0,1,2:T(4,128)} %copy.180) | copy-start | bytes 76
  192.3 11.4 %copy-start.65 = (f32[2,3,1]{0,1,2:T(4,128)S(1)}, f32[2,3,1]{0,1,2:T(4,128)}, u32[]{:S(2)}) copy-start(f32[2,3,1]{0,1,2:T(4,128)} %copy.181) | copy-start | bytes 76
  192.3 11.4 %copy-start.66 = (f32[2,3,1]{0,1,2:T(4,128)S(1)}, f32[2,3,1]{0,1,2:T(4,128)}, u32[]{:S(2)}) copy-start(f32[2,3,1]{0,1,2:T(4,128)} %copy.182) | copy-start | bytes 76
  192.3 11.4 %copy-start.67 = (f32[2,3,1]{0,1,2:T(4,128)S(1)}, f32[2,3,1]{0,1,2:T(4,128)}, u32[]{:S(2)}) copy-start(f32[2,3,1]{0,1,2:T(4,128)} %copy.183) | copy-start | bytes 76
  192.3 11.4 %copy-start.68 = (f32[2,3,1]{0,1,2:T(4,128)S(1)}, f32[2,3,1]{0,1,2:T(4,128)}, u32[]{:S(2)}) copy-start(f32[2,3,1]{0,1,2:T(4,128)} %copy.166) | copy-start | bytes 76
  192.3 11.4 %copy-start.69 = (f32[2,3,1]{0,1,2:T(4,128)S(1)}, f32[2,3,1]{0,1,2:T(4,128)}, u32[]{:S(2)}) copy-start(f32[2,3,1]{0,1,2:T(4,128)} %copy.184) | copy-start | bytes 76
  192.3 11.4 %copy-start.70 = (f32[2,3,1]{0,1,2:T(4,128)S(1)}, f32[2,3,1]{0,1,2:T(4,128)}, u32[]{:S(2)}) copy-start(f32[2,3,1]{0,1,2:T(4,128)} %copy.185) | copy-start | bytes 76
  207.4 3.0 collective-permute-start
  208.9 3.8 %collective-permute-start.1 = (f32[32,16,256]{2,1,0:T(8,128)S(1)}, f32[32,16,256]{2,1,0:T(8,128)S(1)}, u32[]{:S(2)}, u32[]{:S(2)}) collective-permute-start(f32[32,16,256]{2,1,0:T(8,128)S(1)} %get-tuple-element.44), channel_id=1, source_target_pairs={{1,0},{2,1},{3,2},{4,3},{5,4},{6,5},{7,6},{9,8},{10,9},{11,10},{12... | collective-permute-start | bytes 1572872 | tf_op jit(solution)/shard_map/ppermute | solution.py:77
  (45 other events, 173.9 us)
Sparse Core Ops, SparseCore 0:
  249.5 51.4 all-reduce.4
where the time goes:
time: 316 us; the launch traced here: 311 us
  waiting for transfers between devices  108 us (34%)
  local copies, waits for them, and re-layouts  59.3 us (19%)
  matrix products  39.1 us (12%)
  blocking collectives  36.4 us (12%)
  other arithmetic  28.5 us (9%)
  between operations  21.6 us (7%)
  starting transfers between devices  18.3 us (6%)
    psum x1, waiting for transfers between devices, shards(): summed = lax.psum(logs, 'grp')  51.6 us
    broadcast_in_dim x62, local copies, waits for them, and re-layouts, band(): out = jnp.where(shift == t, taps[..., t, None, None], out)  42.3 us
    all_to_all x1, blocking collectives, shards(): lax.all_to_all(logs.reshape(blocks, cz, py, nx), 'blk', 0, 0, tiled=True)  36.4 us
    all_to_all x1, waiting for transfers between devices, shards(): lax.all_to_all(windows, 'blk', 0, 0, tiled=True).reshape(nz, ext, nx)  32.7 us
    all_to_all x1, waiting for transfers between devices, shards(): got = lax.all_to_all(send, 'blk', 0, 0, tiled=True)  20.7 us
    eq x48, other arithmetic, band(): out = jnp.where(shift == t, taps[..., t, None, None], out)  18.7 us
    dot_general x1, matrix products, shards(): a = jnp.einsum('vrzin,vrnx->vrzix', a, bx, precision=HIGH)  11 us
    dot_general x1, matrix products, shards(): t = jnp.einsum('vrzix,vrnx->vrzin', t, bx, precision=HIGH)  10.7 us
  transfers between devices with their start and end apart: 6, of which 5 were waited for; matrix products, arithmetic and copies ran while one was open for 26% of the time, Pallas kernels for 0%

commit v1 on v0

--- a/solution.py
+++ b/solution.py
@@ -5,6 +5,38 @@
 
 VSLOT = 2
 HIGH = lax.Precision.HIGH
+
+
+def _cover_pieces_all(w_in, dimension_no, original):
+    a_now = w_in.shape
+    spare = w_in.reshape(
+        *a_now[:dimension_no], original, a_now[dimension_no] // original, *a_now[dimension_no + 1 :]
+    )
+    piece_out = jnp.moveaxis(spare, dimension_no, 0)
+    return piece_out
+
+
+def turn_the_edge(buf, dim_at):
+    buf = jnp.moveaxis(buf, 0, dim_at)
+    after = buf.shape
+    low = buf.reshape(*after[:dim_at], after[dim_at] * after[dim_at + 1], *after[dim_at + 2 :])
+    return low
+
+
+def cut_the_hubs(xin, mesh_name, matrix, load):
+    state_next = lax.axis_index(mesh_name)
+    f_next = lax.axis_size(mesh_name)
+    heard, known = (f_next, state_next)
+    upper = _cover_pieces_all(xin, matrix, heard)
+    crops = [upper[known]]
+    for m in [*range(1, heard)]:
+        main = upper[(known + m) % heard]
+        moved = lax.ppermute(main, mesh_name, [(i0, (i0 + m) % heard) for i0 in range(heard)])
+        crops.append(moved)
+    x_next = jnp.stack(crops)
+    upper = x_next[(known - jnp.arange(heard)) % heard]
+    reached = turn_the_edge(upper, load)
+    return reached
 
 
 def band(taps, rows, cols, lead):
@@ -82,7 +114,7 @@
             + jnp.pad(down, ((0, 0), (rest, 0), (0, 0)))
         )
     logs = jnp.log(average)
-    logs = lax.all_to_all(logs.reshape(blocks, cz, py, nx), "blk", 0, 0, tiled=True)
+    logs = cut_the_hubs(logs.reshape(blocks, cz, py, nx), "blk", 0, 0)
     summed = lax.psum(logs, "grp")
     summed = jnp.transpose(summed, (1, 0, 2, 3)).reshape(cz, ny, nx)
     return estimate * jnp.exp(summed / groups)

time: 316 us -> 316 us (level)
  blocking collectives: 36.4 us -> 0 us
  starting transfers between devices: 18.3 us -> 36 us
  waiting for transfers between devices: 108 us -> 123 us
    all_to_all x1 -> x0, blocking collectives: 36.4 us -> none  [shards(): lax.all_to_all(logs.reshape(blocks, cz, py, nx), 'blk', 0, 0, tiled=True)]
    ppermute x0 -> x7, starting transfers between devices: none -> 16.9 us  [cut_the_hubs(): lax.ppermute(main, mesh_name, [(i0, (i0 + m) % heard) for i0 in range(hea...]
    psum x1, waiting for transfers between devices: 51.6 us -> 61 us  [shards(): summed = lax.psum(logs, 'grp')]
    ppermute x0 -> x7, waiting for transfers between devices: none -> 6.16 us  [cut_the_hubs(): lax.ppermute(main, mesh_name, [(i0, (i0 + m) % heard) for i0 in range(hea...]
    unnamed x215 -> x221, local copies, waits for them, and re-layouts: 7.62 us -> 7.77 us
  transfers between devices with their start and end apart: 6 -> 13, of which waited for: 5 -> 6; matrix products, arithmetic and copies ran while one was open for 26% -> 26% of each run, Pallas kernels for 0% -> 0%
where the time goes in v1:
time: 316 us; the launch traced here: 311 us
  waiting for transfers between devices  123 us (39%)
  local copies, waits for them, and re-layouts  62.1 us (20%)
  matrix products  39 us (12%)
  starting transfers between devices  36 us (11%)
  other arithmetic  29.6 us (9%)
  between operations  21.3 us (7%)
    psum x1, waiting for transfers between devices, shards(): summed = lax.psum(logs, 'grp')  61 us
    broadcast_in_dim x62, local copies, waits for them, and re-layouts, band(): out = jnp.where(shift == t, taps[..., t, None, None], out)  42.3 us
    all_to_all x1, waiting for transfers between devices, shards(): lax.all_to_all(windows, 'blk', 0, 0, tiled=True).reshape(nz, ext, nx)  32.6 us
    all_to_all x1, waiting for transfers between devices, shards(): got = lax.all_to_all(send, 'blk', 0, 0, tiled=True)  20.6 us
    eq x48, other arithmetic, band(): out = jnp.where(shift == t, taps[..., t, None, None], out)  18.7 us
    ppermute x7, starting transfers between devices, cut_the_hubs(): lax.ppermute(main, mesh_name, [(i0, (i0 + m) % heard) for i0 in range(hea...  16.9 us
    dot_general x1, matrix products, shards(): a = jnp.einsum('vrzin,vrnx->vrzix', a, bx, precision=HIGH)  10.8 us
    dot_general x1, matrix products, shards(): t = jnp.einsum('vrzix,vrnx->vrzin', t, bx, precision=HIGH)  10.7 us
  transfers between devices with their start and end apart: 13, of which 6 were waited for; matrix products, arithmetic and copies ran while one was open for 26% of the time, Pallas kernels for 0%

profile of v1, /device:TPU:0, one launch (start us, length us, event | category | flops | bytes accessed | tf_op | source)
XLA Modules:
  0.0 311.2 jit_solution(16551723360989452251)
XLA Ops:
  7.4 1.4 fusion.251
  12.4 0.8 constant_dynamic-slice_fusion.7
  13.1 0.8 constant_dynamic-slice_fusion.5
  15.1 6.4 %all-to-all-start = ((s32[8,4,2]{1,2,0:T(2,128)}), s32[8,4,2]{1,2,0:T(2,128)S(1)}, u32[]{:S(2)}, u32[]{:S(2)}) async-start(s32[8,4,2]{1,2,0:T(2,128)} %copy.106), calls=%async_computation | async-start | bytes 16384 | tf_op jit(solution)/shard_map/all_to_all | solution.py:86
  21.4 0.7 constant_dynamic-slice_fusion.11
  30.9 0.7 constant_dynamic-slice_fusion.1
  32.0 0.8 fusion.160
  32.8 0.8 fusion.178
  33.6 0.8 fusion.196
  34.3 0.8 fusion.214
  62.3 0.7 copy.210
  67.1 0.7 copy.217
  69.9 0.7 copy.221
  77.4 1.3 constant_dynamic-slice_fusion.3
  79.7 1.6 copy.110
  83.9 5.1 %all-to-all-start.1 = ((bf16[32,2,32,256]{3,2,1,0:T(8,128)(2,1)}), bf16[32,2,32,256]{3,2,1,0:T(8,128)(2,1)S(1)}, u32[]{:S(2)}, u32[]{:S(2)}) async-start(bf16[32,2,32,256]{3,2,1,0:T(8,128)(2,1)} %copy.110), calls=%async_computation.1 | async-start | bytes 2097152 | tf_op jit(solution)/shard_map/all_to_all | solution.py:85
  89.0 0.7 fusion.17
  89.8 0.7 bitcast_dynamic-update-slice_fusion.5
  90.5 0.7 bitcast_dynamic-update-slice_fusion.4
  91.2 0.7 bitcast_dynamic-update-slice_fusion.3
  92.0 0.8 bitcast_dynamic-update-slice_fusion.2
  92.7 0.7 bitcast_dynamic-update-slice_fusion.1
  93.4 0.7 bitcast_dynamic-update-slice_fusion
  94.2 0.7 fusion.19
  94.9 20.6 %all-to-all-done.1 = bf16[32,2,32,256]{3,2,1,0:T(8,128)(2,1)S(1)} async-done(((bf16[32,2,32,256]{3,2,1,0:T(8,128)(2,1)}), bf16[32,2,32,256]{3,2,1,0:T(8,128)(2,1)S(1)}, u32[]{:S(2)}, u32[]{:S(2)}) %all-to-all-start.1) | async-done | bytes 1048608 | tf_op jit(solution)/shard_map/all_to_all | solution.py:85
  115.6 1.0 copy-done.2
  116.5 3.6 %all-to-all-start.2 = ((f32[8,4,64,256]{3,2,1,0:T(8,128)}), f32[8,4,64,256]{3,2,1,0:T(8,128)S(1)}, u32[]{:S(2)}, u32[]{:S(2)}) async-start(f32[8,4,64,256]{3,2,1,0:T(8,128)} %fusion.19), calls=%async_computation.2 | async-start | bytes 4194304 | tf_op jit(solution)/shard_map/all_to_all | solution.py:76
  122.3 0.7 fusion.24
  123.0 0.7 fusion.26
  123.7 0.7 fusion.28
  124.4 0.7 fusion.30
  125.8 0.7 fusion.34
  126.5 0.7 fusion.36
  127.3 0.7 fusion.38
  128.0 0.7 fusion.40
  128.7 0.7 fusion.42
  129.4 0.7 fusion.44
  130.1 0.7 fusion.46
  130.8 0.7 fusion.48
  132.2 1.4 eq.740
  133.5 2.9 fusion.14
  136.5 32.6 %all-to-all-done.2 = f32[8,4,64,256]{3,2,1,0:T(8,128)S(1)} async-done(((f32[8,4,64,256]{3,2,1,0:T(8,128)}), f32[8,4,64,256]{3,2,1,0:T(8,128)S(1)}, u32[]{:S(2)}, u32[]{:S(2)}) %all-to-all-start.2) | async-done | bytes 2097184 | tf_op jit(solution)/shard_map/all_to_all | solution.py:76
  169.3 4.2 %convolution_bitcast_fusion = f32[2,3,32,32,256]{4,3,2,1,0:T(8,128)S(1)} fusion(f32[32,64,256,1,1]{2,1,0,4,3:T(8,128)S(1)} %bitcast.208, f32[2,3]{0,1:T(4,128)} %bitcast.271, pred[32,64]{1,0:T(8,128)(4,1)S(1)} %get-tuple-element.129, f32[2,3]{0,1:T(4,128)} %bitcast.269, pred[32,64]{1,0:T(8,128)(4,1)S(1)} %get-tuple-element.130, f32[2,3]{0,1:T(4,128)} %bitcast.267, ...), kind=kOutput, calls=%fused_computation.5 | convolution fusion | flops 604360704 | bytes 8452840 | tf_op jit(solution)/shard_map/zmx,vrim->vrzix/dot_general | solution.py:96
  174.0 10.7 %fusion.2 = f32[2,3,32,32,256]{4,2,1,3,0:T(8,128)S(1)} fusion(f32[2,3,32,32,256]{4,3,2,1,0:T(8,128)S(1)} %convolution_bitcast_fusion, f32[2,3]{0,1:T(4,128)} %bitcast.334, pred[256,256]{1,0:T(8,128)(4,1)S(1)} %get-tuple-element.159, f32[2,3]{0,1:T(4,128)} %bitcast.332, pred[256,256]{1,0:T(8,128)(4,1)S(1)} %get-tuple-element.160, f32[2,3]{0,1:T(4,128)} %bitcast.330, ...), kind=kOutput, calls=%fused_computation.3 | convolution fusion | flops 2428108800 | bytes 14615272 | tf_op jit(solution)/shard_map/vrzix,vrnx->vrzin/dot_general | solution.py:97
  185.1 3.3 %fusion.51 = f32[2,32,32,256,1]{3,1,4,2,0:T(8,128)S(1)} fusion(f32[2,3,32,32,256]{4,2,1,3,0:T(8,128)S(1)} %fusion.2, f32[2,3]{1,0:T(2,128)} %get-tuple-element.34, f32[2,3]{1,0:T(2,128)} %get-tuple-element.35, f32[2,3]{1,0:T(2,128)} %get-tuple-element.33, f32[2,3]{1,0:T(2,128)} %get-tuple-element.32, f32[2,3]{1,0:T(2,128)} %get-tuple-element.31, ...), kind=kOutput, calls=%fused_computation.84 | convolution fusion | flops 302180352 | bytes 8421096 | tf_op jit(solution)/shard_map/vrzin,vrpz->vpin/dot_general | solution.py:98
  188.6 2.9 fusion.4
  191.9 10.8 %fusion = f32[2,3,32,32,256]{4,3,0,2,1:T(8,128)S(1)} fusion(f32[2,3,32,32,256]{4,2,3,1,0:T(8,128)S(1)} %fusion.4, f32[2,3]{0,1:T(4,128)} %bitcast.335, f32[2,3]{0,1:T(4,128)} %bitcast.333, f32[2,3]{0,1:T(4,128)} %bitcast.331, f32[2,3]{0,1:T(4,128)} %bitcast.329, f32[2,3]{0,1:T(4,128)} %bitcast.327, f32[2,3]{0,1:T(4,128)} %bitcast.325, f32[2,3]{0,1:T(4,128)} %bitcast.323, ...), kind=kOutput, calls=%fused_computation.1 | convolution fusion | flops 2428108800 | bytes 14615272 | tf_op jit(solution)/shard_map/vrzin,vrnx->vrzix/dot_general | solution.py:101
  203.1 3.6 %convolution_bitcast_fusion.1 = f32[32,64,256]{2,1,0:T(8,128)S(1)} fusion(f32[2,3,32,32,256]{4,3,0,2,1:T(8,128)S(1)} %fusion, f32[2]{0:T(128)} %pad_maximum_fusion.3, f32[2,3]{0,1:T(4,128)} %bitcast.272, f32[2,3]{0,1:T(4,128)} %bitcast.270, f32[2,3]{0,1:T(4,128)} %bitcast.268, f32[2,3]{0,1:T(4,128)} %bitcast.266, f32[2,3]{0,1:T(4,128)} %bitcast.250, ...), kind=kOutput, calls=%fused_computation.10 | convolution fusion | flops 604372992 | bytes 8452848 | tf_op jit(solution)/shard_map/vrzix,vrim->zmx/dot_general | solution.py:102
  206.8 1.1 fusion.255
  207.8 2.2 collective-permute-start
  210.1 1.3 collective-permute-start.1
  211.5 2.7 collective-permute-done.1
  214.2 1.4 fusion.10
  215.7 6.0 %collective-permute-start.2 = (f32[1,4,32,256]{3,2,1,0:T(8,128)S(1)}, f32[1,4,32,256]{3,2,1,0:T(8,128)S(1)}, u32[]{:S(2)}, u32[]{:S(2)}) collective-permute-start(f32[1,4,32,256]{3,2,1,0:T(8,128)S(1)} %get-tuple-element.51), channel_id=1, source_target_pairs={{0,1},{1,2},{2,3},{3,4},{4,5},{5,6},{6,7},{7,0},{8,9},{9,10},{10,1... | collective-permute-start | bytes 393224 | tf_op jit(solution)/shard_map/ppermute | solution.py:34
  221.7 0.8 collective-permute-start.3
  222.5 2.9 collective-permute-start.4
  225.7 2.3 collective-permute-start.6
  228.0 2.9 collective-permute-start.7
  230.8 1.9 collective-permute-start.8
  232.7 6.0 %collective-permute-done.4 = f32[1,4,32,256]{3,2,1,0:T(8,128)S(1)} collective-permute-done((f32[1,4,32,256]{3,2,1,0:T(8,128)S(1)}, f32[1,4,32,256]{3,2,1,0:T(8,128)S(1)}, u32[]{:S(2)}, u32[]{:S(2)}) %collective-permute-start.4) | collective-permute-done | bytes 131104 | tf_op jit(solution)/shard_map/ppermute | solution.py:34
  239.0 1.6 gather_fusion
  240.6 61.0 %all-reduce.5.cloned.1.call-done = f32[8,4,32,256]{3,2,1,0:T(8,128)} async-done(((f32[8,4,32,256]{3,2,1,0:T(8,128)}), f32[8,4,32,256]{3,2,1,0:T(8,128)}) %all-reduce.5.cloned.1.call-update) | async-done | bytes 1048592 | tf_op jit(solution)/shard_map/psum | solution.py:118
  301.6 1.4 exponential_bitcast_fusion
  303.1 1.1 bitcast_multiply_fusion
  (345 shorter events, 57.4 us)
Async XLA Ops:
  15.1 68.2 %all-to-all-start = ((s32[8,4,2]{1,2,0:T(2,128)}), s32[8,4,2]{1,2,0:T(2,128)S(1)}, u32[]{:S(2)}, u32[]{:S(2)}) async-start(s32[8,4,2]{1,2,0:T(2,128)} %copy.106), calls=%async_computation | async-start | bytes 16384 | tf_op jit(solution)/shard_map/all_to_all | solution.py:86
  83.9 31.7 %all-to-all-start.1 = ((bf16[32,2,32,256]{3,2,1,0:T(8,128)(2,1)}), bf16[32,2,32,256]{3,2,1,0:T(8,128)(2,1)S(1)}, u32[]{:S(2)}, u32[]{:S(2)}) async-start(bf16[32,2,32,256]{3,2,1,0:T(8,128)(2,1)} %copy.110), calls=%async_computation.1 | async-start | bytes 2097152 | tf_op jit(solution)/shard_map/all_to_all | solution.py:85
  116.5 52.6 %all-to-all-start.2 = ((f32[8,4,64,256]{3,2,1,0:T(8,128)}), f32[8,4,64,256]{3,2,1,0:T(8,128)S(1)}, u32[]{:S(2)}, u32[]{:S(2)}) async-start(f32[8,4,64,256]{3,2,1,0:T(8,128)} %fusion.19), calls=%async_computation.2 | async-start | bytes 4194304 | tf_op jit(solution)/shard_map/all_to_all | solution.py:76
  120.1 181.5 %all-reduce.5.cloned.1.call-start = ((), (), s32[]{:S(2)}) async-start(), calls=%async_computation.3 | async-start | bytes 2097152 | tf_op jit(solution)/shard_map/psum | solution.py:118
  120.7 10.9 %copy-start.57 = (s32[8,4,2]{1,2,0:T(2,128)S(1)}, s32[8,4,2]{1,2,0:T(2,128)}, u32[]{:S(2)}) copy-start(s32[8,4,2]{1,2,0:T(2,128)} %copy-done.56) | copy-start | bytes 772
  173.9 10.9 %copy-start.71 = (f32[2,3]{1,0:T(2,128)S(1)}, f32[2,3]{1,0:T(2,128)}, u32[]{:S(2)}) copy-start(f32[2,3]{1,0:T(2,128)} %get-tuple-element.5) | copy-start | bytes 76
  173.9 10.9 %copy-start.72 = (f32[2,3]{1,0:T(2,128)S(1)}, f32[2,3]{1,0:T(2,128)}, u32[]{:S(2)}) copy-start(f32[2,3]{1,0:T(2,128)} %get-tuple-element.6) | copy-start | bytes 76
  173.9 10.9 %copy-start.73 = (f32[2,3]{1,0:T(2,128)S(1)}, f32[2,3]{1,0:T(2,128)}, u32[]{:S(2)}) copy-start(f32[2,3]{1,0:T(2,128)} %get-tuple-element.7) | copy-start | bytes 76
  173.9 10.9 %copy-start.74 = (f32[2,3]{1,0:T(2,128)S(1)}, f32[2,3]{1,0:T(2,128)}, u32[]{:S(2)}) copy-start(f32[2,3]{1,0:T(2,128)} %get-tuple-element.8) | copy-start | bytes 76
  173.9 10.9 %copy-start.75 = (f32[2,3]{1,0:T(2,128)S(1)}, f32[2,3]{1,0:T(2,128)}, u32[]{:S(2)}) copy-start(f32[2,3]{1,0:T(2,128)} %get-tuple-element.9) | copy-start | bytes 76
  173.9 10.9 %copy-start.76 = (f32[2,3]{1,0:T(2,128)S(1)}, f32[2,3]{1,0:T(2,128)}, u32[]{:S(2)}) copy-start(f32[2,3]{1,0:T(2,128)} %get-tuple-element.10) | copy-start | bytes 76
  173.9 10.9 %copy-start.77 = (f32[2,3]{1,0:T(2,128)S(1)}, f32[2,3]{1,0:T(2,128)}, u32[]{:S(2)}) copy-start(f32[2,3]{1,0:T(2,128)} %get-tuple-element.11) | copy-start | bytes 76
  174.0 10.9 %copy-start.78 = (f32[2,3]{1,0:T(2,128)S(1)}, f32[2,3]{1,0:T(2,128)}, u32[]{:S(2)}) copy-start(f32[2,3]{1,0:T(2,128)} %get-tuple-element.12) | copy-start | bytes 76
  174.0 10.9 %copy-start.79 = (f32[2,3]{1,0:T(2,128)S(1)}, f32[2,3]{1,0:T(2,128)}, u32[]{:S(2)}) copy-start(f32[2,3]{1,0:T(2,128)} %get-tuple-element.13) | copy-start | bytes 76
  174.0 10.9 %copy-start.80 = (f32[2,3]{1,0:T(2,128)S(1)}, f32[2,3]{1,0:T(2,128)}, u32[]{:S(2)}) copy-start(f32[2,3]{1,0:T(2,128)} %get-tuple-element.14) | copy-start | bytes 76
  174.0 10.9 %copy-start.81 = (f32[2,3]{1,0:T(2,128)S(1)}, f32[2,3]{1,0:T(2,128)}, u32[]{:S(2)}) copy-start(f32[2,3]{1,0:T(2,128)} %get-tuple-element.15) | copy-start | bytes 76
  191.5 11.2 %copy-start.30 = (pred[32,64]{1,0:T(8,128)(4,1)S(1)}, pred[32,64]{1,0:T(8,128)(4,1)}, u32[]{:S(2)}) copy-start(pred[32,64]{1,0:T(8,128)(4,1)} %get-tuple-element.134) | copy-start | bytes 6148
  191.5 11.2 %copy-start.31 = (pred[32,64]{1,0:T(8,128)(4,1)S(1)}, pred[32,64]{1,0:T(8,128)(4,1)}, u32[]{:S(2)}) copy-start(pred[32,64]{1,0:T(8,128)(4,1)} %get-tuple-element.135) | copy-start | bytes 6148
  191.5 11.2 %copy-start.32 = (pred[32,64]{1,0:T(8,128)(4,1)S(1)}, pred[32,64]{1,0:T(8,128)(4,1)}, u32[]{:S(2)}) copy-start(pred[32,64]{1,0:T(8,128)(4,1)} %get-tuple-element.136) | copy-start | bytes 6148
  191.6 11.2 %copy-start.33 = (pred[32,64]{1,0:T(8,128)(4,1)S(1)}, pred[32,64]{1,0:T(8,128)(4,1)}, u32[]{:S(2)}) copy-start(pred[32,64]{1,0:T(8,128)(4,1)} %get-tuple-element.137) | copy-start | bytes 6148
  191.6 11.2 %copy-start.34 = (pred[32,64]{1,0:T(8,128)(4,1)S(1)}, pred[32,64]{1,0:T(8,128)(4,1)}, u32[]{:S(2)}) copy-start(pred[32,64]{1,0:T(8,128)(4,1)} %get-tuple-element.138) | copy-start | bytes 6148
  191.6 11.2 %copy-start.35 = (pred[32,64]{1,0:T(8,128)(4,1)S(1)}, pred[32,64]{1,0:T(8,128)(4,1)}, u32[]{:S(2)}) copy-start(pred[32,64]{1,0:T(8,128)(4,1)} %get-tuple-element.139) | copy-start | bytes 6148
  191.6 11.2 %copy-start.36 = (pred[32,64]{1,0:T(8,128)(4,1)S(1)}, pred[32,64]{1,0:T(8,128)(4,1)}, u32[]{:S(2)}) copy-start(pred[32,64]{1,0:T(8,128)(4,1)} %get-tuple-element.140) | copy-start | bytes 6148
  191.6 11.2 %copy-start.37 = (pred[32,64]{1,0:T(8,128)(4,1)S(1)}, pred[32,64]{1,0:T(8,128)(4,1)}, u32[]{:S(2)}) copy-start(pred[32,64]{1,0:T(8,128)(4,1)} %get-tuple-element.141) | copy-start | bytes 6148
  191.6 11.2 %copy-start.38 = (pred[32,64]{1,0:T(8,128)(4,1)S(1)}, pred[32,64]{1,0:T(8,128)(4,1)}, u32[]{:S(2)}) copy-start(pred[32,64]{1,0:T(8,128)(4,1)} %get-tuple-element.142) | copy-start | bytes 6148
  191.6 11.2 %copy-start.39 = (pred[32,64]{1,0:T(8,128)(4,1)S(1)}, pred[32,64]{1,0:T(8,128)(4,1)}, u32[]{:S(2)}) copy-start(pred[32,64]{1,0:T(8,128)(4,1)} %get-tuple-element.143) | copy-start | bytes 6148
  191.6 11.2 %copy-start.40 = (pred[32,64]{1,0:T(8,128)(4,1)S(1)}, pred[32,64]{1,0:T(8,128)(4,1)}, u32[]{:S(2)}) copy-start(pred[32,64]{1,0:T(8,128)(4,1)} %get-tuple-element.144) | copy-start | bytes 6148
  191.6 11.2 %copy-start.41 = (pred[32,64]{1,0:T(8,128)(4,1)S(1)}, pred[32,64]{1,0:T(8,128)(4,1)}, u32[]{:S(2)}) copy-start(pred[32,64]{1,0:T(8,128)(4,1)} %get-tuple-element.145) | copy-start | bytes 6148
  191.6 11.2 %copy-start.42 = (pred[32,64]{1,0:T(8,128)(4,1)S(1)}, pred[32,64]{1,0:T(8,128)(4,1)}, u32[]{:S(2)}) copy-start(pred[32,64]{1,0:T(8,128)(4,1)} %get-tuple-element.146) | copy-start | bytes 6148
  191.7 11.2 %copy-start.43 = (pred[32,64]{1,0:T(8,128)(4,1)S(1)}, pred[32,64]{1,0:T(8,128)(4,1)}, u32[]{:S(2)}) copy-start(pred[32,64]{1,0:T(8,128)(4,1)} %get-tuple-element.147) | copy-start | bytes 6148
  191.7 11.2 %copy-start.44 = (pred[32,64]{1,0:T(8,128)(4,1)S(1)}, pred[32,64]{1,0:T(8,128)(4,1)}, u32[]{:S(2)}) copy-start(pred[32,64]{1,0:T(8,128)(4,1)} %get-tuple-element.148) | copy-start | bytes 6148
  191.7 11.2 %copy-start.45 = (pred[32,64]{1,0:T(8,128)(4,1)S(1)}, pred[32,64]{1,0:T(8,128)(4,1)}, u32[]{:S(2)}) copy-start(pred[32,64]{1,0:T(8,128)(4,1)} %get-tuple-element.149) | copy-start | bytes 6148
  191.7 11.2 %copy-start.46 = (pred[32,64]{1,0:T(8,128)(4,1)S(1)}, pred[32,64]{1,0:T(8,128)(4,1)}, u32[]{:S(2)}) copy-start(pred[32,64]{1,0:T(8,128)(4,1)} %get-tuple-element.150) | copy-start | bytes 6148
  191.7 11.2 %copy-start.47 = (pred[32,64]{1,0:T(8,128)(4,1)S(1)}, pred[32,64]{1,0:T(8,128)(4,1)}, u32[]{:S(2)}) copy-start(pred[32,64]{1,0:T(8,128)(4,1)} %get-tuple-element.151) | copy-start | bytes 6148
  191.7 11.2 %copy-start.48 = (pred[32,64]{1,0:T(8,128)(4,1)S(1)}, pred[32,64]{1,0:T(8,128)(4,1)}, u32[]{:S(2)}) copy-start(pred[32,64]{1,0:T(8,128)(4,1)} %get-tuple-element.152) | copy-start | bytes 6148
  191.7 11.2 %copy-start.49 = (pred[32,64]{1,0:T(8,128)(4,1)S(1)}, pred[32,64]{1,0:T(8,128)(4,1)}, u32[]{:S(2)}) copy-start(pred[32,64]{1,0:T(8,128)(4,1)} %get-tuple-element.153) | copy-start | bytes 6148
  191.7 11.2 %copy-start.50 = (pred[32,64]{1,0:T(8,128)(4,1)S(1)}, pred[32,64]{1,0:T(8,128)(4,1)}, u32[]{:S(2)}) copy-start(pred[32,64]{1,0:T(8,128)(4,1)} %get-tuple-element.154) | copy-start | bytes 6148
  191.7 11.2 %copy-start.51 = (pred[32,64]{1,0:T(8,128)(4,1)S(1)}, pred[32,64]{1,0:T(8,128)(4,1)}, u32[]{:S(2)}) copy-start(pred[32,64]{1,0:T(8,128)(4,1)} %get-tuple-element.155) | copy-start | bytes 6148
  191.7 11.2 %copy-start.52 = (pred[32,64]{1,0:T(8,128)(4,1)S(1)}, pred[32,64]{1,0:T(8,128)(4,1)}, u32[]{:S(2)}) copy-start(pred[32,64]{1,0:T(8,128)(4,1)} %get-tuple-element.156) | copy-start | bytes 6148
  191.8 11.2 %copy-start.53 = (pred[32,64]{1,0:T(8,128)(4,1)S(1)}, pred[32,64]{1,0:T(8,128)(4,1)}, u32[]{:S(2)}) copy-start(pred[32,64]{1,0:T(8,128)(4,1)} %get-tuple-element.157) | copy-start | bytes 6148
  191.8 11.2 %copy-start.54 = (pred[32,64]{1,0:T(8,128)(4,1)S(1)}, pred[32,64]{1,0:T(8,128)(4,1)}, u32[]{:S(2)}) copy-start(pred[32,64]{1,0:T(8,128)(4,1)} %get-tuple-element.158) | copy-start | bytes 6148
  191.8 11.2 %copy-start.55 = (pred[32,64]{1,0:T(8,128)(4,1)S(1)}, pred[32,64]{1,0:T(8,128)(4,1)}, u32[]{:S(2)}) copy-start(pred[32,64]{1,0:T(8,128)(4,1)} %fusion.126) | copy-start | bytes 6148
  191.8 11.2 %copy-start.58 = (f32[2,3,1]{0,1,2:T(4,128)S(1)}, f32[2,3,1]{0,1,2:T(4,128)}, u32[]{:S(2)}) copy-start(f32[2,3,1]{0,1,2:T(4,128)} %copy.174) | copy-start | bytes 76
  191.8 11.2 %copy-start.59 = (f32[2,3,1]{0,1,2:T(4,128)S(1)}, f32[2,3,1]{0,1,2:T(4,128)}, u32[]{:S(2)}) copy-start(f32[2,3,1]{0,1,2:T(4,128)} %copy.175) | copy-start | bytes 76
  191.8 11.2 %copy-start.60 = (f32[2,3,1]{0,1,2:T(4,128)S(1)}, f32[2,3,1]{0,1,2:T(4,128)}, u32[]{:S(2)}) copy-start(f32[2,3,1]{0,1,2:T(4,128)} %copy.176) | copy-start | bytes 76
  191.8 11.2 %copy-start.61 = (f32[2,3,1]{0,1,2:T(4,128)S(1)}, f32[2,3,1]{0,1,2:T(4,128)}, u32[]{:S(2)}) copy-start(f32[2,3,1]{0,1,2:T(4,128)} %copy.177) | copy-start | bytes 76
  191.8 11.2 %copy-start.62 = (f32[2,3,1]{0,1,2:T(4,128)S(1)}, f32[2,3,1]{0,1,2:T(4,128)}, u32[]{:S(2)}) copy-start(f32[2,3,1]{0,1,2:T(4,128)} %copy.178) | copy-start | bytes 76
  191.8 11.2 %copy-start.63 = (f32[2,3,1]{0,1,2:T(4,128)S(1)}, f32[2,3,1]{0,1,2:T(4,128)}, u32[]{:S(2)}) copy-start(f32[2,3,1]{0,1,2:T(4,128)} %copy.179) | copy-start | bytes 76
  191.8 11.2 %copy-start.64 = (f32[2,3,1]{0,1,2:T(4,128)S(1)}, f32[2,3,1]{0,1,2:T(4,128)}, u32[]{:S(2)}) copy-start(f32[2,3,1]{0,1,2:T(4,128)} %copy.180) | copy-start | bytes 76
  191.9 11.2 %copy-start.65 = (f32[2,3,1]{0,1,2:T(4,128)S(1)}, f32[2,3,1]{0,1,2:T(4,128)}, u32[]{:S(2)}) copy-start(f32[2,3,1]{0,1,2:T(4,128)} %copy.181) | copy-start | bytes 76
  191.9 11.2 %copy-start.66 = (f32[2,3,1]{0,1,2:T(4,128)S(1)}, f32[2,3,1]{0,1,2:T(4,128)}, u32[]{:S(2)}) copy-start(f32[2,3,1]{0,1,2:T(4,128)} %copy.182) | copy-start | bytes 76
  191.9 11.2 %copy-start.67 = (f32[2,3,1]{0,1,2:T(4,128)S(1)}, f32[2,3,1]{0,1,2:T(4,128)}, u32[]{:S(2)}) copy-start(f32[2,3,1]{0,1,2:T(4,128)} %copy.183) | copy-start | bytes 76
  191.9 11.2 %copy-start.68 = (f32[2,3,1]{0,1,2:T(4,128)S(1)}, f32[2,3,1]{0,1,2:T(4,128)}, u32[]{:S(2)}) copy-start(f32[2,3,1]{0,1,2:T(4,128)} %copy.166) | copy-start | bytes 76
  191.9 11.2 %copy-start.69 = (f32[2,3,1]{0,1,2:T(4,128)S(1)}, f32[2,3,1]{0,1,2:T(4,128)}, u32[]{:S(2)}) copy-start(f32[2,3,1]{0,1,2:T(4,128)} %copy.184) | copy-start | bytes 76
  191.9 11.2 %copy-start.70 = (f32[2,3,1]{0,1,2:T(4,128)S(1)}, f32[2,3,1]{0,1,2:T(4,128)}, u32[]{:S(2)}) copy-start(f32[2,3,1]{0,1,2:T(4,128)} %copy.185) | copy-start | bytes 76
  207.8 3.6 %collective-permute-start = (f32[32,16,256]{2,1,0:T(8,128)}, f32[32,16,256]{2,1,0:T(8,128)}, u32[]{:S(2)}, u32[]{:S(2)}) collective-permute-start(f32[32,16,256]{2,1,0:T(8,128)} %get-tuple-element.43), channel_id=1, source_target_pairs={{0,1},{1,2},{2,3},{3,4},{4,5},{5,6},{6,7},{8,9},{9,10},{10,11},{11... | collective-permute-start | bytes 1572872 | tf_op jit(solution)/shard_map/ppermute | solution.py:108
  210.1 4.1 %collective-permute-start.1 = (f32[32,16,256]{2,1,0:T(8,128)}, f32[32,16,256]{2,1,0:T(8,128)}, u32[]{:S(2)}, u32[]{:S(2)}) collective-permute-start(f32[32,16,256]{2,1,0:T(8,128)} %get-tuple-element.44), channel_id=1, source_target_pairs={{1,0},{2,1},{3,2},{4,3},{5,4},{6,5},{7,6},{9,8},{10,9},{11,10},{12... | collective-permute-start | bytes 1572872 | tf_op jit(solution)/shard_map/ppermute | solution.py:109
  215.7 12.3 %collective-permute-start.2 = (f32[1,4,32,256]{3,2,1,0:T(8,128)S(1)}, f32[1,4,32,256]{3,2,1,0:T(8,128)S(1)}, u32[]{:S(2)}, u32[]{:S(2)}) collective-permute-start(f32[1,4,32,256]{3,2,1,0:T(8,128)S(1)} %get-tuple-element.51), channel_id=1, source_target_pairs={{0,1},{1,2},{2,3},{3,4},{4,5},{5,6},{6,7},{7,0},{8,9},{9,10},{10,1... | collective-permute-start | bytes 393224 | tf_op jit(solution)/shard_map/ppermute | solution.py:34
  221.7 9.2 %collective-permute-start.3 = (f32[1,4,32,256]{3,2,1,0:T(8,128)S(1)}, f32[1,4,32,256]{3,2,1,0:T(8,128)S(1)}, u32[]{:S(2)}, u32[]{:S(2)}) collective-permute-start(f32[1,4,32,256]{3,2,1,0:T(8,128)S(1)} %get-tuple-element.50), channel_id=1, source_target_pairs={{0,2},{1,3},{2,4},{3,5},{4,6},{5,7},{6,0},{7,1},{8,10},{9,11},{10,... | collective-permute-start | bytes 393224 | tf_op jit(solution)/shard_map/ppermute | solution.py:34
  222.5 16.2 %collective-permute-start.4 = (f32[1,4,32,256]{3,2,1,0:T(8,128)S(1)}, f32[1,4,32,256]{3,2,1,0:T(8,128)S(1)}, u32[]{:S(2)}, u32[]{:S(2)}) collective-permute-start(f32[1,4,32,256]{3,2,1,0:T(8,128)S(1)} %get-tuple-element.49), channel_id=1, source_target_pairs={{0,3},{1,4},{2,5},{3,6},{4,7},{5,0},{6,1},{7,2},{8,11},{9,12},{10,... | collective-permute-start | bytes 393224 | tf_op jit(solution)/shard_map/ppermute | solution.py:34
  225.4 13.4 %collective-permute-start.5 = (f32[1,4,32,256]{3,2,1,0:T(8,128)S(1)}, f32[1,4,32,256]{3,2,1,0:T(8,128)S(1)}, u32[]{:S(2)}, u32[]{:S(2)}) collective-permute-start(f32[1,4,32,256]{3,2,1,0:T(8,128)S(1)} %get-tuple-element.48), channel_id=1, source_target_pairs={{0,4},{1,5},{2,6},{3,7},{4,0},{5,1},{6,2},{7,3},{8,12},{9,13},{10,... | collective-permute-start | bytes 393224 | tf_op jit(solution)/shard_map/ppermute | solution.py:34
  225.7 13.2 %collective-permute-start.6 = (f32[1,4,32,256]{3,2,1,0:T(8,128)S(1)}, f32[1,4,32,256]{3,2,1,0:T(8,128)S(1)}, u32[]{:S(2)}, u32[]{:S(2)}) collective-permute-start(f32[1,4,32,256]{3,2,1,0:T(8,128)S(1)} %get-tuple-element.47), channel_id=1, source_target_pairs={{0,5},{1,6},{2,7},{3,0},{4,1},{5,2},{6,3},{7,4},{8,13},{9,14},{10,... | collective-permute-start | bytes 393224 | tf_op jit(solution)/shard_map/ppermute | solution.py:34
  228.0 11.0 %collective-permute-start.7 = (f32[1,4,32,256]{3,2,1,0:T(8,128)S(1)}, f32[1,4,32,256]{3,2,1,0:T(8,128)S(1)}, u32[]{:S(2)}, u32[]{:S(2)}) collective-permute-start(f32[1,4,32,256]{3,2,1,0:T(8,128)S(1)} %get-tuple-element.46), channel_id=1, source_target_pairs={{0,6},{1,7},{2,0},{3,1},{4,2},{5,3},{6,4},{7,5},{8,14},{9,15},{10,... | collective-permute-start | bytes 393224 | tf_op jit(solution)/shard_map/ppermute | solution.py:34
  230.8 8.1 %collective-permute-start.8 = (f32[1,4,32,256]{3,2,1,0:T(8,128)S(1)}, f32[1,4,32,256]{3,2,1,0:T(8,128)S(1)}, u32[]{:S(2)}, u32[]{:S(2)}) collective-permute-start(f32[1,4,32,256]{3,2,1,0:T(8,128)S(1)} %get-tuple-element.45), channel_id=1, source_target_pairs={{0,7},{1,0},{2,1},{3,2},{4,3},{5,4},{6,5},{7,6},{8,15},{9,8},{10,9... | collective-permute-start | bytes 393224 | tf_op jit(solution)/shard_map/ppermute | solution.py:34
  (52 other events, 217.8 us)
Sparse Core Ops, SparseCore 0:
  240.7 60.8 all-reduce.4
